TPU v7x, 32 devices: a whole 2x2x4 slice. The times are simulated.
32 devices in a mesh: section: 2 (over core), req: 4 (over z), head: 4 (over y, x).
Axes of the slice: x: 2, y: 2, z: 4, core: 2. Of those that a mesh axis runs over, the one named last changes fastest.
Arguments:
- tokens: bfloat16 [128, 1024], P('req'), may hold values from -60 to 60, as said below
- deal: int32 [128], P('req'), may hold values from 0 to 127, each once
- lengths: int32 [2, 128], P('section', 'req'), may hold values from 2 to 256, as said below
- cache_keys: bfloat16 [2, 128, 256, 1024], P('section', 'req', None, 'head'), may hold values from -1024 to 1024
- cache_values: bfloat16 [2, 128, 256, 1024], P('section', 'req', None, 'head'), may hold values from -6 to 6
- w_qkv: bfloat16 [2, 1024, 3, 1024], P('section', None, None, 'head'), may hold values from -0.1875 to 0.1875
- w_out: bfloat16 [2, 1024, 1024], P('section', 'head'), may hold values from -0.1875 to 0.1875
- attn_gain: float32 [2, 1024], P('section'), may hold values from 0.5 to 1.5
- ffn_gain: float32 [2, 1024], P('section'), may hold values from 0.5 to 1.5
- w_gate: bfloat16 [2, 1024, 45056], P('section', None, ('req', 'head')), may hold values from -0.1875 to 0.1875
- w_up: bfloat16 [2, 1024, 45056], P('section', None, ('req', 'head')), may hold values from -0.1875 to 0.1875
- w_down: bfloat16 [2, 45056, 1024], P('section', ('req', 'head')), may hold values from -0.109375 to 0.109375
- routes: int32 [2, 128, 2], P('section', 'req'), may hold values from 0 to 15, all different within a row; in each aligned block of 16 rows (0 to 15, 16 to 31, ..., all dimensions but the last counted through in order) at most 4 rows name the same one
- gates: bfloat16 [2, 128, 2], P('section', 'req'), may hold values from 0.25 to 1
Outputs:
- layer_out: bfloat16 [2, 128, 1024], P('section', 'req')
Inputs may be any that keep to these rules, and one draw needn't show every extreme that they name: `tokens`: hidden states with row and feature scales that differ. `deal`: each of 0 to 127 appears once. `lengths`: in each layer, one of the 32 slots of each index of req holds a length of exactly 256; the others are anywhere from 2 to 256. `routes`: the two experts of a slot differ; in each aligned block of 16 slots of one layer no expert is named more than 4 times.
All inputs are finite; a program needn't handle non-finite values.
Results may differ from a plain program's by a relative error of at most 0.0053.
Values may be sent and summed in bfloat16 or wider, within the bound.
A program may use at most 128 MiB of HBM per device.

v0:
```python
import math
import jax
import jax.numpy as jnp
from jax import lax
from jax.sharding import PartitionSpec as P

HEAD_DIM = 64
EXPERTS = 16
FF = 2816
MICRO = 2
epsilon = 1e-06


def shifted(x, axis, by):
    size = lax.axis_size(axis)
    pairs = [(i, i + by) for i in range(size) if 0 <= i + by < size]
    return lax.ppermute(x, axis, pairs)


def rms_scale(values, gain_row):
    mean_square = jnp.mean(values * values, axis=-1, keepdims=True)
    return values * lax.rsqrt(mean_square + epsilon) * gain_row


def attend_block(queries, new_keys, new_values, key_cache, value_cache, lengths):
    score_scale = 1.0 / math.sqrt(queries.shape[-1])
    scores = (
        jnp.einsum("bhd,bjhd->bhj", queries, key_cache, preferred_element_type=jnp.float32)
        * score_scale
    )
    own_score = (
        jnp.sum(queries.astype(jnp.float32) * new_keys.astype(jnp.float32), axis=-1) * score_scale
    )
    positions = jnp.arange(key_cache.shape[1], dtype=jnp.int32)
    in_range = positions[None, None, :] < lengths[:, None, None]
    scores = jnp.where(in_range, scores, -jnp.inf)
    peak_score = jnp.maximum(jnp.max(scores, axis=-1), own_score)
    cache_weight = jnp.exp(scores - peak_score[..., None])
    own_weight = jnp.exp(own_score - peak_score)
    denominator = jnp.sum(cache_weight, axis=-1) + own_weight
    cache_prob = (cache_weight / denominator[..., None]).astype(jnp.bfloat16)
    own_prob = (own_weight / denominator).astype(jnp.bfloat16)
    attended = jnp.einsum(
        "bhj,bjhd->bhd", cache_prob, value_cache, preferred_element_type=jnp.float32
    )
    attended = attended + own_prob.astype(jnp.float32)[..., None] * new_values.astype(jnp.float32)
    return attended.astype(jnp.bfloat16)


def on_device(
    tokens,
    deal,
    lengths,
    cache_keys,
    cache_values,
    w_qkv,
    w_out,
    attn_gain,
    ffn_gain,
    w_gate,
    w_up,
    w_down,
    routes,
    gates,
):
    req_count = lax.axis_size("req")
    head_count = lax.axis_size("head")
    section_index = lax.axis_index("section")
    request_slots = tokens.shape[0]
    model_width = tokens.shape[1]
    block_rows = request_slots // MICRO
    unit_count = w_gate.shape[2]
    head_cols = w_out.shape[1]
    heads_here = head_cols // HEAD_DIM
    context = cache_keys.shape[2]
    expert_ids = jnp.arange(EXPERTS, dtype=jnp.int32)
    own_expert = (lax.axis_index("req") * head_count + lax.axis_index("head")) * unit_count // FF
    qkv_weight = w_qkv[0].reshape(model_width, 3 * head_cols)
    everything = lax.all_gather(tokens, "req", axis=0, tiled=True)
    dealt_rows = jnp.take(everything, deal, axis=0)
    results = jnp.zeros((request_slots, model_width), jnp.bfloat16)
    incoming = jnp.zeros((block_rows, model_width), jnp.bfloat16)
    for tick_index in range(MICRO + 1):
        micro_index = tick_index - section_index
        in_window = (micro_index >= 0) & (micro_index < MICRO)
        clamped = jnp.clip(micro_index, 0, MICRO - 1)
        fresh_rows = lax.dynamic_slice_in_dim(dealt_rows, clamped * block_rows, block_rows, 0)
        hidden_in = jnp.where(section_index == 0, fresh_rows, incoming)
        row_start = clamped * block_rows
        lengths_here = lax.dynamic_slice_in_dim(lengths[0], row_start, block_rows, 0)
        key_cache = lax.dynamic_slice_in_dim(cache_keys[0], row_start, block_rows, 0).reshape(
            block_rows, context, heads_here, HEAD_DIM
        )
        value_cache = lax.dynamic_slice_in_dim(cache_values[0], row_start, block_rows, 0).reshape(
            block_rows, context, heads_here, HEAD_DIM
        )
        route_ids = lax.dynamic_slice_in_dim(routes[0], row_start, block_rows, 0)
        gate_vals = lax.dynamic_slice_in_dim(gates[0], row_start, block_rows, 0)
        normed = rms_scale(hidden_in.astype(jnp.float32), attn_gain[0]).astype(jnp.bfloat16)
        projected = jnp.dot(normed, qkv_weight, preferred_element_type=jnp.float32).astype(
            jnp.bfloat16
        )
        queries = projected[:, :head_cols].reshape(block_rows, heads_here, HEAD_DIM)
        new_keys = projected[:, head_cols : 2 * head_cols].reshape(block_rows, heads_here, HEAD_DIM)
        new_values = projected[:, 2 * head_cols :].reshape(block_rows, heads_here, HEAD_DIM)
        attended = attend_block(
            queries, new_keys, new_values, key_cache, value_cache, lengths_here
        ).reshape(block_rows, head_cols)
        partial_value = jnp.dot(attended, w_out[0], preferred_element_type=jnp.float32)
        attention = lax.psum(partial_value, "head")
        residual = hidden_in.astype(jnp.float32) + attention
        normed_ffn = rms_scale(residual, ffn_gain[0]).astype(jnp.bfloat16)
        bf_zero = jnp.zeros((), jnp.bfloat16)
        combine = jnp.sum(
            jnp.where(
                route_ids[:, :, None] == expert_ids[None, None, :], gate_vals[:, :, None], bf_zero
            ),
            axis=1,
        )
        piece_tokens, piece_combine = lax.all_gather(
            (normed_ffn, combine), "req", axis=0, tiled=True
        )
        expert_row_weight = jnp.sum(
            jnp.where(expert_ids[None, :] == own_expert, piece_combine.astype(jnp.float32), 0.0),
            axis=1,
        )
        gate_part = jnp.dot(piece_tokens, w_gate[0], preferred_element_type=jnp.float32)
        up_part = jnp.dot(piece_tokens, w_up[0], preferred_element_type=jnp.float32)
        hidden = (
            expert_row_weight[:, None] * jax.nn.gelu(gate_part, approximate=True) * up_part
        ).astype(jnp.bfloat16)
        partial_terms = jnp.dot(hidden, w_down[0], preferred_element_type=jnp.float32)
        mixture = lax.psum_scatter(partial_terms, "req", scatter_dimension=0, tiled=True)
        mixture = lax.psum(mixture, "head")
        produced = (residual + mixture).astype(jnp.bfloat16)
        updated = lax.dynamic_update_slice_in_dim(results, produced, clamped * block_rows, 0)
        results = jnp.where(in_window, updated, results)
        if tick_index < MICRO:
            incoming = shifted(produced, "section", 1)
    placed = (
        jnp.zeros((request_slots * req_count, model_width), jnp.float32)
        .at[deal]
        .set(results.astype(jnp.float32))
    )
    initial_rows = lax.psum_scatter(
        placed.astype(jnp.bfloat16), "req", scatter_dimension=0, tiled=True
    )
    return initial_rows[None]


def solution(mesh):
    return jax.shard_map(
        on_device,
        mesh=mesh,
        in_specs=(
            P("req", None),
            P("req"),
            P("section", "req"),
            P("section", "req", None, "head"),
            P("section", "req", None, "head"),
            P("section", None, None, "head"),
            P("section", "head", None),
            P("section", None),
            P("section", None),
            P("section", None, ("req", "head")),
            P("section", None, ("req", "head")),
            P("section", ("req", "head"), None),
            P("section", "req", None),
            P("section", "req", None),
        ),
        out_specs=P("section", "req", None),
        check_vma=False,
    )
```

profile of v0, /device:TPU:0, one launch (start us, length us, event | category | flops | bytes accessed | tf_op | source)
XLA Modules:
  0.0 505.5 jit_solution(13057923560571487558)
XLA Ops:
  7.9 15.8 %all_gather.21 = bf16[128,1024]{1,0:T(8,128)(2,1)S(1)} all-gather(bf16[32,1024]{1,0:T(8,128)(2,1)} %param.14), channel_id=1, replica_groups=mesh['section'=2,'req'=4,'head'=4] {'req'}, dimensions={0}, use_global_device_ids=true | all-gather | bytes 327680 | tf_op jit(solution)/shard_map/all_gather | solution.py:79
  27.1 9.2 %constant_dynamic-slice_fusion.2 = (bf16[1,16,256,256]{3,2,1,0:T(8,128)(2,1)}, bf16[1,16,256,256]{3,2,1,0:T(8,128)(2,1)}, bf16[1,16,256,256]{3,2,1,0:T(8,128)(2,...) fusion(bf16[1,32,256,256]{3,2,1,0:T(8,128)(2,1)} %param.18, ...), kind=kLoop, calls=%fused_computation.162 | loop fusion | bytes 25165836 | tf_op jit(solution)/shard_map/dynamic_slice | solution.py:94
  36.3 3.9 copy.78
  43.0 3.9 copy.79
  47.1 2.2 fusion.103
  50.7 13.2 %all_gather.22 = bf16[64,16]{1,0:T(8,128)(2,1)S(1)} all-gather(bf16[16,16]{1,0:T(8,128)(2,1)S(1)} %fusion.130), channel_id=1, replica_groups=mesh['section'=2,'req'=4,'head'=4] {'req'}, dimensions={0}, use_global_device_ids=true | all-gather | bytes 2560 | tf_op jit(solution)/shard_map/all_gather | solution.py:120
  64.0 13.1 %all_gather.24 = bf16[64,16]{1,0:T(8,128)(2,1)S(1)} all-gather(bf16[16,16]{1,0:T(8,128)(2,1)S(1)} %fusion.129), channel_id=1, replica_groups=mesh['section'=2,'req'=4,'head'=4] {'req'}, dimensions={0}, use_global_device_ids=true | all-gather | bytes 2560 | tf_op jit(solution)/shard_map/all_gather | solution.py:120
  77.2 13.1 %all_gather.26 = bf16[64,16]{1,0:T(8,128)(2,1)S(1)} all-gather(bf16[16,16]{1,0:T(8,128)(2,1)S(1)} %fusion.128), channel_id=1, replica_groups=mesh['section'=2,'req'=4,'head'=4] {'req'}, dimensions={0}, use_global_device_ids=true | all-gather | bytes 2560 | tf_op jit(solution)/shard_map/all_gather | solution.py:120
  90.4 3.1 all-reduce.7.cloned.1.call-done
  95.5 13.5 %all_gather.23 = bf16[64,1024]{1,0:T(8,128)(2,1)S(1)} all-gather(bf16[16,1024]{1,0:T(8,128)(2,1)S(1)} %multiply_convert_fusion.2), channel_id=1, replica_groups=mesh['section'=2,'req'=4,'head'=4] {'req'}, dimensions={0}, use_global_device_ids=true | all-gather | bytes 163840 | tf_op jit(solution)/shard_map/all_gather | solution.py:120
  109.0 3.9 fusion.45
  112.9 7.2 %fusion.4 = f32[64,1024]{1,0:T(8,128)} fusion(bf16[1,2816,1024]{2,1,0:T(8,128)(2,1)} %param.25, f32[64,2816]{1,0:T(8,128)S(1)} %fusion.45, bf16[64,1024]{1,0:T(8,128)(2,1)S(1)} %all_gather.23, bf16[1,1024,2816]{2,1,0:T(8,128)(2,1)} %param.24), kind=kOutput, calls=%fused_computation.6 | convolution fusion | flops 738557952 | bytes 12648448 | tf_op jit(solution)/shard_map/dot_general | solution.py:132
  120.1 19.8 %reduce-scatter.5.cloned.1.call-done = f32[16,1024]{1,0:T(8,128)} async-done(((f32[64,1024]{1,0:T(8,128)}), f32[16,1024]{1,0:T(8,128)}) %reduce-scatter.5.cloned.1.call-update) | async-done | bytes 65552 | tf_op jit(solution)/shard_map/reduce_scatter | solution.py:133
  140.0 42.5 %all-reduce.9.cloned.1.call-done = f32[16,1024]{1,0:T(8,128)} async-done(((f32[16,1024]{1,0:T(8,128)}), f32[16,1024]{1,0:T(8,128)}) %all-reduce.9.cloned.1.call-update) | async-done | bytes 65552 | tf_op jit(solution)/shard_map/psum | solution.py:134
  184.8 3.9 copy.80
  188.7 3.9 copy.81
  196.3 2.2 fusion.101
  199.7 41.6 %all-reduce.11.cloned.1.call-done = f32[16,1024]{1,0:T(8,128)} async-done(((f32[16,1024]{1,0:T(8,128)}), f32[16,1024]{1,0:T(8,128)}) %all-reduce.11.cloned.1.call-update) | async-done | bytes 65552 | tf_op jit(solution)/shard_map/psum | solution.py:110
  243.1 13.5 %all_gather.25 = bf16[64,1024]{1,0:T(8,128)(2,1)S(1)} all-gather(bf16[16,1024]{1,0:T(8,128)(2,1)S(1)} %multiply_convert_fusion.1), channel_id=1, replica_groups=mesh['section'=2,'req'=4,'head'=4] {'req'}, dimensions={0}, use_global_device_ids=true | all-gather | bytes 163840 | tf_op jit(solution)/shard_map/all_gather | solution.py:120
  256.6 3.9 fusion.57
  260.5 7.2 %fusion.2 = f32[64,1024]{1,0:T(8,128)} fusion(bf16[1,2816,1024]{2,1,0:T(8,128)(2,1)} %param.25, f32[64,2816]{1,0:T(8,128)S(1)} %fusion.57, bf16[64,1024]{1,0:T(8,128)(2,1)S(1)} %all_gather.25, bf16[1,1024,2816]{2,1,0:T(8,128)(2,1)} %param.24), kind=kOutput, calls=%fused_computation.4 | convolution fusion | flops 738557952 | bytes 12648448 | tf_op jit(solution)/shard_map/dot_general | solution.py:132
  267.7 19.7 %reduce-scatter.7.cloned.1.call-done = f32[16,1024]{1,0:T(8,128)} async-done(((f32[64,1024]{1,0:T(8,128)}), f32[16,1024]{1,0:T(8,128)}) %reduce-scatter.7.cloned.1.call-update) | async-done | bytes 65552 | tf_op jit(solution)/shard_map/reduce_scatter | solution.py:133
  287.5 42.6 %all-reduce.13.cloned.1.call-done = f32[16,1024]{1,0:T(8,128)} async-done(((f32[16,1024]{1,0:T(8,128)}), f32[16,1024]{1,0:T(8,128)}) %all-reduce.13.cloned.1.call-update) | async-done | bytes 65552 | tf_op jit(solution)/shard_map/psum | solution.py:134
  332.6 3.9 copy.82
  336.5 3.9 copy.83
  346.0 41.6 %all-reduce.15.cloned.1.call-done = f32[16,1024]{1,0:T(8,128)} async-done(((f32[16,1024]{1,0:T(8,128)}), f32[16,1024]{1,0:T(8,128)}) %all-reduce.15.cloned.1.call-update) | async-done | bytes 65552 | tf_op jit(solution)/shard_map/psum | solution.py:110
  389.5 13.5 %all_gather.27 = bf16[64,1024]{1,0:T(8,128)(2,1)S(1)} all-gather(bf16[16,1024]{1,0:T(8,128)(2,1)S(1)} %multiply_convert_fusion), channel_id=1, replica_groups=mesh['section'=2,'req'=4,'head'=4] {'req'}, dimensions={0}, use_global_device_ids=true | all-gather | bytes 163840 | tf_op jit(solution)/shard_map/all_gather | solution.py:120
  403.0 3.9 fusion.69
  406.9 7.2 %fusion = f32[64,1024]{1,0:T(8,128)} fusion(bf16[1,2816,1024]{2,1,0:T(8,128)(2,1)} %param.25, f32[64,2816]{1,0:T(8,128)S(1)} %fusion.69, bf16[64,1024]{1,0:T(8,128)(2,1)S(1)} %all_gather.27, bf16[1,1024,2816]{2,1,0:T(8,128)(2,1)} %param.24), kind=kOutput, calls=%fused_computation.2 | convolution fusion | flops 738557952 | bytes 12648448 | tf_op jit(solution)/shard_map/dot_general | solution.py:132
  414.1 19.8 %reduce-scatter.9.cloned.1.call-done = f32[16,1024]{1,0:T(8,128)} async-done(((f32[64,1024]{1,0:T(8,128)}), f32[16,1024]{1,0:T(8,128)}) %reduce-scatter.9.cloned.1.call-update) | async-done | bytes 65552 | tf_op jit(solution)/shard_map/reduce_scatter | solution.py:133
  434.0 42.5 %all-reduce.17.cloned.1.call-done = f32[16,1024]{1,0:T(8,128)} async-done(((f32[16,1024]{1,0:T(8,128)}), f32[16,1024]{1,0:T(8,128)}) %all-reduce.17.cloned.1.call-update) | async-done | bytes 65552 | tf_op jit(solution)/shard_map/psum | solution.py:134
  479.0 19.7 %reduce-scatter.11.cloned.1.call-done = bf16[32,1024]{1,0:T(8,128)(2,1)} async-done(((bf16[128,1024]{1,0:T(8,128)(2,1)}), bf16[32,1024]{1,0:T(8,128)(2,1)}) %reduce-scatter.11.cloned.1.call-update) | async-done | bytes 65552 | tf_op jit(solution)/shard_map/reduce_scatter | solution.py:145
  (136 shorter events, 32.6 us)
Async XLA Ops:
  6.5 43.0 %copy-start = (bf16[1,256,1024]{2,1,0:T(8,128)(2,1)S(1)}, bf16[1,256,1024]{2,1,0:T(8,128)(2,1)}, u32[]{:S(2)}) copy-start(bf16[1,256,1024]{2,1,0:T(8,128)(2,1)} %param.20) | copy-start | bytes 1572868
  6.5 87.0 %all-reduce.7.cloned.1.call-start = ((), (), s32[]{:S(2)}) async-start(), calls=%async_computation.4 | async-start | bytes 131072 | tf_op jit(solution)/shard_map/psum | solution.py:110
  7.9 18.4 %copy-start.5 = (f32[1,1024]{1,0:T(1,128)S(1)}, f32[1,1024]{1,0:T(1,128)}, u32[]{:S(2)}) copy-start(f32[1,1024]{1,0:T(1,128)} %param.21) | copy-start | bytes 12292
  36.3 3.9 copy-start.8
  47.0 3.5 copy-start.7
  47.0 3.6 copy-start.9
  47.0 47.6 %copy-start.6 = (f32[1,1024]{1,0:T(1,128)S(1)}, f32[1,1024]{1,0:T(1,128)}, u32[]{:S(2)}) copy-start(f32[1,1024]{1,0:T(1,128)} %param.22) | copy-start | bytes 12292
  50.4 89.5 %reduce-scatter.5.cloned.1.call-start = ((), (), s32[]{:S(2)}) async-start(), calls=%async_computation.5 | async-start | bytes 327680 | tf_op jit(solution)/shard_map/reduce_scatter | solution.py:133
  112.9 69.7 %copy-start.2 = (f32[16,1024]{1,0:T(8,128)S(1)}, f32[16,1024]{1,0:T(8,128)}, u32[]{:S(2)}) copy-start(f32[16,1024]{1,0:T(8,128)} %all-reduce.7.cloned.1.call-done) | copy-start | bytes 196612
  120.1 62.4 %all-reduce.9.cloned.1.call-start = ((), (), s32[]{:S(2)}) async-start(), calls=%async_computation.6 | async-start | bytes 131072 | tf_op jit(solution)/shard_map/psum | solution.py:134
  139.9 101.3 %all-reduce.11.cloned.1.call-start = ((), (), s32[]{:S(2)}) async-start(), calls=%async_computation.7 | async-start | bytes 131072 | tf_op jit(solution)/shard_map/psum | solution.py:110
  183.4 9.3 %collective-permute-start = (bf16[16,1024]{1,0:T(8,128)(2,1)S(1)}, bf16[16,1024]{1,0:T(8,128)(2,1)S(1)}, u32[]{:S(2)}, u32[]{:S(2)}) collective-permute-start(bf16[16,1024]{1,0:T(8,128)(2,1)S(1)} %get-tuple-element.15), channel_id=1, source_target_pairs={{0,16},{1,17},{2,18},{3,19},{4,20},{5,21},{6,22},{7,23},{8,24},{9,... | collective-permute-start | bytes 98312 | tf_op jit(solution)/shard_map/ppermute | solution.py:17
  199.6 87.9 %reduce-scatter.7.cloned.1.call-start = ((), (), s32[]{:S(2)}) async-start(), calls=%async_computation.8 | async-start | bytes 327680 | tf_op jit(solution)/shard_map/reduce_scatter | solution.py:133
  260.5 69.7 %copy-start.4 = (f32[16,1024]{1,0:T(8,128)S(1)}, f32[16,1024]{1,0:T(8,128)}, u32[]{:S(2)}) copy-start(f32[16,1024]{1,0:T(8,128)} %all-reduce.11.cloned.1.call-done) | copy-start | bytes 196612
  267.7 62.5 %all-reduce.13.cloned.1.call-start = ((), (), s32[]{:S(2)}) async-start(), calls=%async_computation.9 | async-start | bytes 131072 | tf_op jit(solution)/shard_map/psum | solution.py:134
  287.5 100.1 %all-reduce.15.cloned.1.call-start = ((), (), s32[]{:S(2)}) async-start(), calls=%async_computation.10 | async-start | bytes 131072 | tf_op jit(solution)/shard_map/psum | solution.py:110
  331.0 9.4 %collective-permute-start.1 = (bf16[16,1024]{1,0:T(8,128)(2,1)S(1)}, bf16[16,1024]{1,0:T(8,128)(2,1)S(1)}, u32[]{:S(2)}, u32[]{:S(2)}) collective-permute-start(bf16[16,1024]{1,0:T(8,128)(2,1)S(1)} %get-tuple-element.11), channel_id=1, source_target_pairs={{0,16},{1,17},{2,18},{3,19},{4,20},{5,21},{6,22},{7,23},{8,24},{9,... | collective-permute-start | bytes 98312 | tf_op jit(solution)/shard_map/ppermute | solution.py:17
  341.1 3.2 copy-start.1
  346.0 87.9 %reduce-scatter.9.cloned.1.call-start = ((), (), s32[]{:S(2)}) async-start(), calls=%async_computation.11 | async-start | bytes 327680 | tf_op jit(solution)/shard_map/reduce_scatter | solution.py:133
  406.9 69.6 %copy-start.3 = (f32[16,1024]{1,0:T(8,128)S(1)}, f32[16,1024]{1,0:T(8,128)}, u32[]{:S(2)}) copy-start(f32[16,1024]{1,0:T(8,128)} %all-reduce.15.cloned.1.call-done) | copy-start | bytes 196612
  414.1 62.4 %all-reduce.17.cloned.1.call-start = ((), (), s32[]{:S(2)}) async-start(), calls=%async_computation.12 | async-start | bytes 131072 | tf_op jit(solution)/shard_map/psum | solution.py:134
  433.9 64.8 %reduce-scatter.11.cloned.1.call-start = ((), (), s32[]{:S(2)}) async-start(), calls=%async_computation.13 | async-start | bytes 327680 | tf_op jit(solution)/shard_map/reduce_scatter | solution.py:145
Sparse Core Ops, SparseCore 0:
  50.5 43.0 all-reduce.6
  120.2 19.6 reduce-scatter.4
  142.8 39.6 all-reduce.8
  199.7 41.4 all-reduce.10
  267.8 19.6 reduce-scatter.6
  290.4 39.7 all-reduce.12
  346.1 41.4 all-reduce.14
  414.2 19.6 reduce-scatter.8
  436.8 39.6 all-reduce.16
  479.1 19.5 reduce-scatter.10
where the time goes:
time: 507 us; the launch traced here: 506 us
  waiting for transfers between devices  293 us (58%)
  blocking collectives  95.8 us (19%)
  matrix products  48.3 us (10%)
  local copies, waits for them, and re-layouts  37.2 us (7%)
  other arithmetic  14 us (3%)
  between operations  13.9 us (3%)
    psum x3, waiting for transfers between devices, on_device(): mixture = lax.psum(mixture, 'head')  128 us
    psum x3, waiting for transfers between devices, on_device(): attention = lax.psum(partial_value, 'head')  86.3 us
    all_gather x6, blocking collectives, on_device(): lax.all_gather((normed_ffn, combine), 'req', axis=0, tiled=True)  79.9 us
    reduce_scatter x3, waiting for transfers between devices, on_device(): lax.psum_scatter(partial_terms, 'req', scatter_dimension=0, tiled=True)  59.3 us
    unnamed x27, local copies, waits for them, and re-layouts  25.3 us
    dot_general x3, matrix products, on_device(): jnp.dot(hidden, w_down[0], preferred_element_type=jnp.float32)  21.5 us
    reduce_scatter x1, waiting for transfers between devices, on_device(): lax.psum_scatter(placed.astype(jnp.bfloat16), 'req', scatter_dimension=0,...  19.7 us
    all_gather x1, blocking collectives, on_device(): everything = lax.all_gather(tokens, 'req', axis=0, tiled=True)  15.8 us
  transfers between devices with their start and end apart: 12, of which 10 were waited for; matrix products, arithmetic and copies ran while one was open for 3% of the time, Pallas kernels for 0%

commit v1 on v0

--- a/solution.py
+++ b/solution.py
@@ -9,6 +9,10 @@
 FF = 2816
 MICRO = 2
 epsilon = 1e-06
+
+
+def _lay_masks(inputs):
+    return lax.all_gather(inputs, "head").sum(axis=0)
 
 
 def shifted(x, axis, by):
@@ -131,7 +135,7 @@
         ).astype(jnp.bfloat16)
         partial_terms = jnp.dot(hidden, w_down[0], preferred_element_type=jnp.float32)
         mixture = lax.psum_scatter(partial_terms, "req", scatter_dimension=0, tiled=True)
-        mixture = lax.psum(mixture, "head")
+        mixture = _lay_masks(mixture)
         produced = (residual + mixture).astype(jnp.bfloat16)
         updated = lax.dynamic_update_slice_in_dim(results, produced, clamped * block_rows, 0)
         results = jnp.where(in_window, updated, results)

time: 507 us -> 398 us (0.79)
  waiting for transfers between devices: 293 us -> 158 us
  blocking collectives: 95.8 us -> 124 us
    psum x3 -> x0, waiting for transfers between devices: 128 us -> none  [on_device(): mixture = lax.psum(mixture, 'head')]
    all_gather x0 -> x3, blocking collectives: none -> 28.1 us  [_lay_masks(): return lax.all_gather(inputs, 'head').sum(axis=0)]
    psum x3, waiting for transfers between devices: 86.3 us -> 81.1 us  [on_device(): attention = lax.psum(partial_value, 'head')]
    unnamed x27 -> x25, local copies, waits for them, and re-layouts: 25.3 us -> 25.3 us
  transfers between devices with their start and end apart: 12 -> 9, of which waited for: 10 -> 7; matrix products, arithmetic and copies ran while one was open for 3% -> 4% of each run, Pallas kernels for 0% -> 0%
where the time goes in v1:
time: 398 us; the launch traced here: 397 us
  waiting for transfers between devices  158 us (40%)
  blocking collectives  124 us (31%)
  matrix products  49.7 us (12%)
  local copies, waits for them, and re-layouts  37.2 us (9%)
  between operations  13.9 us (3%)
  other arithmetic  11.5 us (3%)
    psum x3, waiting for transfers between devices, on_device(): attention = lax.psum(partial_value, 'head')  81.1 us
    all_gather x6, blocking collectives, on_device(): lax.all_gather((normed_ffn, combine), 'req', axis=0, tiled=True)  79.9 us
    reduce_scatter x3, waiting for transfers between devices, on_device(): lax.psum_scatter(partial_terms, 'req', scatter_dimension=0, tiled=True)  59.3 us
    all_gather x3, blocking collectives, _lay_masks(): return lax.all_gather(inputs, 'head').sum(axis=0)  28.1 us
    unnamed x25, local copies, waits for them, and re-layouts  25.3 us
    dot_general x3, matrix products, on_device(): jnp.dot(hidden, w_down[0], preferred_element_type=jnp.float32)  21.5 us
    reduce_scatter x1, waiting for transfers between devices, on_device(): lax.psum_scatter(placed.astype(jnp.bfloat16), 'req', scatter_dimension=0,...  17.2 us
    all_gather x1, blocking collectives, on_device(): everything = lax.all_gather(tokens, 'req', axis=0, tiled=True)  15.8 us
  transfers between devices with their start and end apart: 9, of which 7 were waited for; matrix products, arithmetic and copies ran while one was open for 4% of the time, Pallas kernels for 0%

profile of v1, /device:TPU:0, one launch (start us, length us, event | category | flops | bytes accessed | tf_op | source)
XLA Modules:
  0.0 396.9 jit_solution(4974789988614014061)
XLA Ops:
  7.9 15.8 %all_gather.39 = bf16[128,1024]{1,0:T(8,128)(2,1)S(1)} all-gather(bf16[32,1024]{1,0:T(8,128)(2,1)} %param.14), channel_id=1, replica_groups=mesh['section'=2,'req'=4,'head'=4] {'req'}, dimensions={0}, use_global_device_ids=true | all-gather | bytes 327680 | tf_op jit(solution)/shard_map/all_gather | solution.py:83
  27.1 9.2 %constant_dynamic-slice_fusion.2 = (bf16[1,16,256,256]{3,2,1,0:T(8,128)(2,1)}, bf16[1,16,256,256]{3,2,1,0:T(8,128)(2,1)}, bf16[1,16,256,256]{3,2,1,0:T(8,128)(2,...) fusion(bf16[1,32,256,256]{3,2,1,0:T(8,128)(2,1)} %param.18, ...), kind=kLoop, calls=%fused_computation.162 | loop fusion | bytes 25165836 | tf_op jit(solution)/shard_map/dynamic_slice | solution.py:98
  36.3 3.9 copy.78
  43.0 3.9 copy.79
  47.1 2.2 fusion.103
  50.7 13.2 %all_gather.40 = bf16[64,16]{1,0:T(8,128)(2,1)S(1)} all-gather(bf16[16,16]{1,0:T(8,128)(2,1)S(1)} %fusion.130), channel_id=1, replica_groups=mesh['section'=2,'req'=4,'head'=4] {'req'}, dimensions={0}, use_global_device_ids=true | all-gather | bytes 2560 | tf_op jit(solution)/shard_map/all_gather | solution.py:124
  64.0 13.1 %all_gather.44 = bf16[64,16]{1,0:T(8,128)(2,1)S(1)} all-gather(bf16[16,16]{1,0:T(8,128)(2,1)S(1)} %fusion.129), channel_id=1, replica_groups=mesh['section'=2,'req'=4,'head'=4] {'req'}, dimensions={0}, use_global_device_ids=true | all-gather | bytes 2560 | tf_op jit(solution)/shard_map/all_gather | solution.py:124
  77.2 13.1 %all_gather.48 = bf16[64,16]{1,0:T(8,128)(2,1)S(1)} all-gather(bf16[16,16]{1,0:T(8,128)(2,1)S(1)} %fusion.128), channel_id=1, replica_groups=mesh['section'=2,'req'=4,'head'=4] {'req'}, dimensions={0}, use_global_device_ids=true | all-gather | bytes 2560 | tf_op jit(solution)/shard_map/all_gather | solution.py:124
  90.4 3.1 all-reduce.4.cloned.1.call-done
  95.5 13.5 %all_gather.41 = bf16[64,1024]{1,0:T(8,128)(2,1)S(1)} all-gather(bf16[16,1024]{1,0:T(8,128)(2,1)S(1)} %multiply_convert_fusion.2), channel_id=1, replica_groups=mesh['section'=2,'req'=4,'head'=4] {'req'}, dimensions={0}, use_global_device_ids=true | all-gather | bytes 163840 | tf_op jit(solution)/shard_map/all_gather | solution.py:124
  109.0 3.9 fusion.45
  112.9 7.2 %fusion.4 = f32[64,1024]{1,0:T(8,128)} fusion(bf16[1,2816,1024]{2,1,0:T(8,128)(2,1)} %param.25, f32[64,2816]{1,0:T(8,128)S(1)} %fusion.45, bf16[64,1024]{1,0:T(8,128)(2,1)S(1)} %all_gather.41, bf16[1,1024,2816]{2,1,0:T(8,128)(2,1)} %param.24), kind=kOutput, calls=%fused_computation.6 | convolution fusion | flops 738557952 | bytes 12648448 | tf_op jit(solution)/shard_map/dot_general | solution.py:136
  120.1 19.8 %reduce-scatter.5.cloned.1.call-done = f32[16,1024]{1,0:T(8,128)} async-done(((f32[64,1024]{1,0:T(8,128)}), f32[16,1024]{1,0:T(8,128)}) %reduce-scatter.5.cloned.1.call-update) | async-done | bytes 65552 | tf_op jit(solution)/shard_map/reduce_scatter | solution.py:137
  139.9 9.4 %all-gather = f32[64,1024]{1,0:T(8,128)S(1)} all-gather(f32[16,1024]{1,0:T(8,128)} %reduce-scatter.5.cloned.1.call-done), channel_id=2, replica_groups=mesh['section'=2,'req'=4,'head'=4] {'head'}, dimensions={0}, use_global_device_ids=true | all-gather | bytes 327680 | tf_op jit(solution)/shard_map/all_gather | solution.py:15
  150.7 3.9 copy.80
  154.6 3.9 copy.81
  162.2 2.2 fusion.101
  165.5 39.0 %all-reduce.6.cloned.1.call-done = f32[16,1024]{1,0:T(8,128)} async-done(((f32[16,1024]{1,0:T(8,128)}), f32[16,1024]{1,0:T(8,128)}) %all-reduce.6.cloned.1.call-update) | async-done | bytes 65552 | tf_op jit(solution)/shard_map/psum | solution.py:114
  206.4 13.5 %all_gather.45 = bf16[64,1024]{1,0:T(8,128)(2,1)S(1)} all-gather(bf16[16,1024]{1,0:T(8,128)(2,1)S(1)} %multiply_convert_fusion.1), channel_id=1, replica_groups=mesh['section'=2,'req'=4,'head'=4] {'req'}, dimensions={0}, use_global_device_ids=true | all-gather | bytes 163840 | tf_op jit(solution)/shard_map/all_gather | solution.py:124
  219.9 3.9 fusion.57
  223.8 7.2 %fusion.2 = f32[64,1024]{1,0:T(8,128)} fusion(bf16[1,2816,1024]{2,1,0:T(8,128)(2,1)} %param.25, f32[64,2816]{1,0:T(8,128)S(1)} %fusion.57, bf16[64,1024]{1,0:T(8,128)(2,1)S(1)} %all_gather.45, bf16[1,1024,2816]{2,1,0:T(8,128)(2,1)} %param.24), kind=kOutput, calls=%fused_computation.4 | convolution fusion | flops 738557952 | bytes 12648448 | tf_op jit(solution)/shard_map/dot_general | solution.py:136
  231.0 19.8 %reduce-scatter.7.cloned.1.call-done = f32[16,1024]{1,0:T(8,128)} async-done(((f32[64,1024]{1,0:T(8,128)}), f32[16,1024]{1,0:T(8,128)}) %reduce-scatter.7.cloned.1.call-update) | async-done | bytes 65552 | tf_op jit(solution)/shard_map/reduce_scatter | solution.py:137
  250.8 9.4 %all-gather.1 = f32[64,1024]{1,0:T(8,128)S(1)} all-gather(f32[16,1024]{1,0:T(8,128)} %reduce-scatter.7.cloned.1.call-done), channel_id=3, replica_groups=mesh['section'=2,'req'=4,'head'=4] {'head'}, dimensions={0}, use_global_device_ids=true | all-gather | bytes 327680 | tf_op jit(solution)/shard_map/all_gather | solution.py:15
  261.7 3.9 copy.82
  265.6 3.9 copy.83
  276.6 38.9 %all-reduce.8.cloned.1.call-done = f32[16,1024]{1,0:T(8,128)} async-done(((f32[16,1024]{1,0:T(8,128)}), f32[16,1024]{1,0:T(8,128)}) %all-reduce.8.cloned.1.call-update) | async-done | bytes 65552 | tf_op jit(solution)/shard_map/psum | solution.py:114
  317.4 13.5 %all_gather.49 = bf16[64,1024]{1,0:T(8,128)(2,1)S(1)} all-gather(bf16[16,1024]{1,0:T(8,128)(2,1)S(1)} %multiply_convert_fusion), channel_id=1, replica_groups=mesh['section'=2,'req'=4,'head'=4] {'req'}, dimensions={0}, use_global_device_ids=true | all-gather | bytes 163840 | tf_op jit(solution)/shard_map/all_gather | solution.py:124
  330.9 3.9 fusion.69
  334.8 7.2 %fusion = f32[64,1024]{1,0:T(8,128)} fusion(bf16[1,2816,1024]{2,1,0:T(8,128)(2,1)} %param.25, f32[64,2816]{1,0:T(8,128)S(1)} %fusion.69, bf16[64,1024]{1,0:T(8,128)(2,1)S(1)} %all_gather.49, bf16[1,1024,2816]{2,1,0:T(8,128)(2,1)} %param.24), kind=kOutput, calls=%fused_computation.2 | convolution fusion | flops 738557952 | bytes 12648448 | tf_op jit(solution)/shard_map/dot_general | solution.py:136
  342.0 19.8 %reduce-scatter.9.cloned.1.call-done = f32[16,1024]{1,0:T(8,128)} async-done(((f32[64,1024]{1,0:T(8,128)}), f32[16,1024]{1,0:T(8,128)}) %reduce-scatter.9.cloned.1.call-update) | async-done | bytes 65552 | tf_op jit(solution)/shard_map/reduce_scatter | solution.py:137
  361.8 9.4 %all-gather.2 = f32[64,1024]{1,0:T(8,128)S(1)} all-gather(f32[16,1024]{1,0:T(8,128)} %reduce-scatter.9.cloned.1.call-done), channel_id=4, replica_groups=mesh['section'=2,'req'=4,'head'=4] {'head'}, dimensions={0}, use_global_device_ids=true | all-gather | bytes 327680 | tf_op jit(solution)/shard_map/all_gather | solution.py:15
  372.8 17.2 %reduce-scatter.11.cloned.1.call-done = bf16[32,1024]{1,0:T(8,128)(2,1)} async-done(((bf16[128,1024]{1,0:T(8,128)(2,1)}), bf16[32,1024]{1,0:T(8,128)(2,1)}) %reduce-scatter.11.cloned.1.call-update) | async-done | bytes 65552 | tf_op jit(solution)/shard_map/reduce_scatter | solution.py:149
  (131 shorter events, 31.2 us)
Async XLA Ops:
  6.5 43.0 %copy-start = (bf16[1,256,1024]{2,1,0:T(8,128)(2,1)S(1)}, bf16[1,256,1024]{2,1,0:T(8,128)(2,1)}, u32[]{:S(2)}) copy-start(bf16[1,256,1024]{2,1,0:T(8,128)(2,1)} %param.20) | copy-start | bytes 1572868
  6.5 87.0 %all-reduce.4.cloned.1.call-start = ((), (), s32[]{:S(2)}) async-start(), calls=%async_computation.4 | async-start | bytes 131072 | tf_op jit(solution)/shard_map/psum | solution.py:114
  7.9 18.4 %copy-start.4 = (f32[1,1024]{1,0:T(1,128)S(1)}, f32[1,1024]{1,0:T(1,128)}, u32[]{:S(2)}) copy-start(f32[1,1024]{1,0:T(1,128)} %param.21) | copy-start | bytes 12292
  36.3 3.9 copy-start.7
  47.0 3.5 copy-start.6
  47.0 3.6 copy-start.8
  47.0 47.6 %copy-start.5 = (f32[1,1024]{1,0:T(1,128)S(1)}, f32[1,1024]{1,0:T(1,128)}, u32[]{:S(2)}) copy-start(f32[1,1024]{1,0:T(1,128)} %param.22) | copy-start | bytes 12292
  50.4 89.5 %reduce-scatter.5.cloned.1.call-start = ((), (), s32[]{:S(2)}) async-start(), calls=%async_computation.5 | async-start | bytes 327680 | tf_op jit(solution)/shard_map/reduce_scatter | solution.py:137
  112.9 36.4 %copy-start.1 = (f32[16,1024]{1,0:T(8,128)S(1)}, f32[16,1024]{1,0:T(8,128)}, u32[]{:S(2)}) copy-start(f32[16,1024]{1,0:T(8,128)} %all-reduce.4.cloned.1.call-done) | copy-start | bytes 196612
  120.1 84.5 %all-reduce.6.cloned.1.call-start = ((), (), s32[]{:S(2)}) async-start(), calls=%async_computation.6 | async-start | bytes 131072 | tf_op jit(solution)/shard_map/psum | solution.py:114
  149.3 9.2 %collective-permute-start = (bf16[16,1024]{1,0:T(8,128)(2,1)S(1)}, bf16[16,1024]{1,0:T(8,128)(2,1)S(1)}, u32[]{:S(2)}, u32[]{:S(2)}) collective-permute-start(bf16[16,1024]{1,0:T(8,128)(2,1)S(1)} %get-tuple-element.15), channel_id=1, source_target_pairs={{0,16},{1,17},{2,18},{3,19},{4,20},{5,21},{6,22},{7,23},{8,24},{9,... | collective-permute-start | bytes 98312 | tf_op jit(solution)/shard_map/ppermute | solution.py:21
  165.5 85.3 %reduce-scatter.7.cloned.1.call-start = ((), (), s32[]{:S(2)}) async-start(), calls=%async_computation.7 | async-start | bytes 327680 | tf_op jit(solution)/shard_map/reduce_scatter | solution.py:137
  223.8 36.4 %copy-start.3 = (f32[16,1024]{1,0:T(8,128)S(1)}, f32[16,1024]{1,0:T(8,128)}, u32[]{:S(2)}) copy-start(f32[16,1024]{1,0:T(8,128)} %all-reduce.6.cloned.1.call-done) | copy-start | bytes 196612
  231.0 84.5 %all-reduce.8.cloned.1.call-start = ((), (), s32[]{:S(2)}) async-start(), calls=%async_computation.8 | async-start | bytes 131072 | tf_op jit(solution)/shard_map/psum | solution.py:114
  260.2 9.3 %collective-permute-start.1 = (bf16[16,1024]{1,0:T(8,128)(2,1)S(1)}, bf16[16,1024]{1,0:T(8,128)(2,1)S(1)}, u32[]{:S(2)}, u32[]{:S(2)}) collective-permute-start(bf16[16,1024]{1,0:T(8,128)(2,1)S(1)} %get-tuple-element.11), channel_id=1, source_target_pairs={{0,16},{1,17},{2,18},{3,19},{4,20},{5,21},{6,22},{7,23},{8,24},{9,... | collective-permute-start | bytes 98312 | tf_op jit(solution)/shard_map/ppermute | solution.py:21
  276.5 85.3 %reduce-scatter.9.cloned.1.call-start = ((), (), s32[]{:S(2)}) async-start(), calls=%async_computation.9 | async-start | bytes 327680 | tf_op jit(solution)/shard_map/reduce_scatter | solution.py:137
  334.8 36.4 %copy-start.2 = (f32[16,1024]{1,0:T(8,128)S(1)}, f32[16,1024]{1,0:T(8,128)}, u32[]{:S(2)}) copy-start(f32[16,1024]{1,0:T(8,128)} %all-reduce.8.cloned.1.call-done) | copy-start | bytes 196612
  342.0 48.1 %reduce-scatter.11.cloned.1.call-start = ((), (), s32[]{:S(2)}) async-start(), calls=%async_computation.10 | async-start | bytes 327680 | tf_op jit(solution)/shard_map/reduce_scatter | solution.py:149
Sparse Core Ops, SparseCore 0:
  50.5 43.0 all-reduce.3
  120.2 19.6 reduce-scatter.4
  165.6 38.8 all-reduce.5
  231.1 19.6 reduce-scatter.6
  276.6 38.8 all-reduce.7
  342.1 19.6 reduce-scatter.8
  372.9 17.0 reduce-scatter.10
